TPU v7x, 256 devices: a whole 4x4x8 slice. The times are simulated.
256 devices in a mesh: leaf: 32 (over y, z), panel: 8 (over x, core).
Axes of the slice: x: 4, y: 4, z: 8, core: 2. Of those that a mesh axis runs over, the one named last changes fastest.
Arguments:
- child_front: float32 [32, 2, 8, 128, 2048], P('leaf', None, 'panel'), as said below
- parent_entries: float32 [32, 4, 8, 128, 512], P('leaf', None, 'panel'), as said below
- parent_of: int32 [32], replicated, may hold values from 0 to 31
- owner_slot: int32 [32], replicated, may hold values from 0 to 31, each once
- front_blocks: int32 [32], replicated, may hold values from 8 to 32, as said below
- block_lists: int32 [32, 8], replicated, may hold values from 0 to 31, as said below
Outputs:
- child_factor: float32 [32, 2, 8, 128, 1024], P('leaf', None, 'panel')
- parent_factor: float32 [32, 4, 8, 128, 512], P('leaf', None, 'panel')
Inputs may be any that keep to these rules, and one draw needn't show every extreme that they name: `front_blocks`: each entry is a multiple of the panel axis size; the largest equals 32. `block_lists`: the entries of a row are distinct, each below front_blocks of the child's parent, and entry k leaves the same remainder as k when divided by the panel axis size. `child_front`: symmetric, with a positive definite leading block of every front. `parent_entries`: the leading 512 rows form a symmetric positive definite block.
All inputs are finite; a program needn't handle non-finite values.
Results may differ from a plain program's by a relative error of at most 0.00044.
Values may be sent and summed in bfloat16 or wider, within the bound.
No kernel may reach another device: no remote copies, remote signals or barrier semaphores. Data moves between devices by JAX's collectives and lax.ppermute only.
A program may use at most 128 MiB of HBM per device.

v0:
```python
import jax
import jax.numpy as jnp
from jax import lax
from jax.sharding import PartitionSpec as P

BLK = 128
PANEL = 512
WC = 2048
PC = 1024
CBB = 8


def place_columns(block_rows, block_map):
    count_in = block_rows.shape[0]
    row_slots = block_rows.shape[1]
    pivot_blocks = PANEL // BLK
    onehot = (block_map[:, :, None] == jnp.arange(pivot_blocks)[None, None, :]).astype(jnp.bfloat16)
    split_blocks = block_rows.reshape(count_in, row_slots, BLK, CBB, BLK)
    placed = jnp.einsum(
        "muvkc,mkb->muvbc", split_blocks, onehot, preferred_element_type=jnp.float32
    )
    return placed.reshape(count_in, row_slots, BLK, PANEL)


def place_rows(assembled, placed, block_map, destination, panel_count, panel_index, leaf_index):
    count_in = placed.shape[0]
    row_slots = placed.shape[1]
    parent_slots = assembled.shape[0]
    grouped = block_map.reshape(count_in, row_slots, panel_count)
    pick = (jnp.arange(panel_count) == panel_index).astype(jnp.int32)
    row_blocks = jnp.sum(grouped * pick[None, None, :], axis=2)
    target = row_blocks[:, :, None] // panel_count == jnp.arange(parent_slots)[None, None, :]
    target = jnp.logical_and(target, (destination == leaf_index)[:, None, None]).astype(jnp.float32)
    return assembled + jnp.einsum("muvx,mut->tvx", placed, target, precision=lax.Precision.HIGHEST)


def on_device(child_front, parent_entries, parent_of, owner_slot, front_blocks, block_lists):
    panel_count = lax.axis_size("panel")
    panel_index = lax.axis_index("panel")
    leaf_index = lax.axis_index("leaf")
    row_slots = child_front.shape[1]
    parent_slots = parent_entries.shape[1]
    local_rows = child_front.reshape(row_slots * BLK, WC)
    factors = []
    for first_col in range(0, PC, PANEL):
        trailing = first_col + PANEL
        column = local_rows[:, first_col:trailing]
        gathered = lax.all_gather(
            column.reshape(row_slots, 1, BLK, PANEL), "panel", axis=1, tiled=True
        )
        gathered = gathered.reshape(WC, PANEL)
        pivot_block = jnp.linalg.cholesky(gathered[first_col:trailing])
        all_rows = jax.scipy.linalg.solve_triangular(pivot_block, gathered.T, lower=True).T
        all_rows = jnp.where(jnp.arange(WC)[:, None] >= first_col, all_rows, 0.0)
        own_rows = lax.dynamic_slice_in_dim(
            all_rows.reshape(row_slots, panel_count, BLK, PANEL), panel_index, 1, 1
        )
        own_rows = own_rows.reshape(row_slots * BLK, PANEL)
        update = jnp.dot(own_rows, all_rows[trailing:].T, precision=lax.Precision.HIGHEST)
        local_rows = jnp.concatenate(
            [local_rows[:, :trailing], local_rows[:, trailing:] - update], axis=1
        )
        factors.append(own_rows)
    child_factor = jnp.concatenate(factors, axis=1).reshape(1, row_slots, 1, BLK, PC)
    first_cb = PC // (BLK * panel_count)
    contribution = local_rows.reshape(row_slots, BLK, WC)[first_cb:, :, PC:].astype(jnp.bfloat16)
    parent_hits = (parent_of[:, None] == jnp.arange(owner_slot.shape[0])[None, :]).astype(jnp.int32)
    slot_of_child = jnp.sum(parent_hits * owner_slot[None, :], axis=1)
    live_mine = jnp.sum(jnp.where(owner_slot == leaf_index, front_blocks, 0))
    entries = parent_entries.reshape(parent_slots, BLK, PANEL)
    global_block = jnp.arange(parent_slots) * panel_count + panel_index
    initial = jnp.where((global_block < live_mine)[:, None, None], entries, 0.0)
    placed = place_columns(
        lax.all_gather(contribution[None], "leaf", axis=0, tiled=True), block_lists
    )
    assembled = place_rows(
        initial, placed, block_lists, slot_of_child, panel_count, panel_index, leaf_index
    )
    stacked = lax.all_gather(assembled[0], "panel", axis=0, tiled=True)
    pivot_block = jnp.linalg.cholesky(stacked[:PANEL])
    parent_rows = assembled.reshape(parent_slots * BLK, PANEL)
    parent_factor = jax.scipy.linalg.solve_triangular(pivot_block, parent_rows.T, lower=True).T
    return (child_factor, parent_factor.reshape(1, parent_slots, 1, BLK, PANEL))


def solution(mesh):
    in_specs = (
        P("leaf", None, "panel", None, None),
        P("leaf", None, "panel", None, None),
        P(),
        P(),
        P(),
        P(),
    )
    out_specs = (P("leaf", None, "panel", None, None), P("leaf", None, "panel", None, None))
    return jax.shard_map(
        on_device, mesh=mesh, in_specs=in_specs, out_specs=out_specs, check_vma=False
    )
```

profile of v0, /device:TPU:39, one launch (start us, length us, event | category | flops | bytes accessed | tf_op | source)
XLA Modules:
  0.0 734.8 jit_solution(10436099563935229929)
XLA Ops:
  9.2 37.1 %all-gather.7.cloned.1.call-done = f32[2,8,128,512]{3,2,0,1:T(8,128)} async-done(((f32[2,1,128,512]{3,2,0,1:T(8,128)}), f32[2,8,128,512]{3,2,0,1:T(8,128)}) %all-gather.7.cloned.1.call-update) | async-done | bytes 4194320 | tf_op jit(solution)/shard_map/all_gather | solution.py:48
  59.6 11.7 %cholesky.374 = f32[128,128]{1,0:T(8,128)S(1)} custom-call(f32[128,128]{1,0:T(8,128)S(1)} %cholesky.586), custom_call_target="Cholesky" | custom-call | tf_op jit(solution)/shard_map/jit(cholesky)/cholesky | solution.py:52
  82.0 11.9 %cholesky.393 = f32[128,128]{1,0:T(8,128)S(1)} custom-call(f32[128,128]{1,0:T(8,128)S(1)} %cholesky.590), custom_call_target="Cholesky" | custom-call | tf_op jit(solution)/shard_map/jit(cholesky)/cholesky | solution.py:52
  93.9 9.8 %custom-call.36 = f32[1,128,128]{1,2,0:T(8,128)S(1)} custom-call(f32[1,128,128]{2,1,0:T(8,128)S(1)} %get-tuple-element.100), custom_call_target="InvertDiagBlocksLowerTriangular" | custom-call | tf_op jit(solution)/shard_map/jit(cholesky)/cholesky | solution.py:52
  104.4 11.7 %cholesky.414 = f32[128,128]{1,0:T(8,128)S(1)} custom-call(f32[128,128]{1,0:T(8,128)S(1)} %cholesky.595), custom_call_target="Cholesky" | custom-call | tf_op jit(solution)/shard_map/jit(cholesky)/cholesky | solution.py:52
  127.2 12.1 %cholesky.431 = f32[128,128]{1,0:T(8,128)S(1)} custom-call(f32[128,128]{1,0:T(8,128)S(1)} %convolution_subtract_fusion.15), custom_call_target="Cholesky" | custom-call | tf_op jit(solution)/shard_map/jit(cholesky)/cholesky | solution.py:52
  151.4 39.3 %custom-call.38 = f32[4,128,128]{1,2,0:T(8,128)S(1)} custom-call(f32[4,128,128]{2,1,0:T(8,128)S(1)} %get-tuple-element.26), custom_call_target="InvertDiagBlocksLowerTriangular" | custom-call | tf_op jit(solution)/shard_map/jit(_solve_triangular)/triangular_solve | solution.py:53
  210.5 33.7 %all-gather.9.cloned.1.call-done = f32[2,8,128,512]{3,2,0,1:T(8,128)} async-done(((f32[2,1,128,512]{3,2,0,1:T(8,128)}), f32[2,8,128,512]{3,2,0,1:T(8,128)}) %all-gather.9.cloned.1.call-update) | async-done | bytes 4194320 | tf_op jit(solution)/shard_map/all_gather | solution.py:48
  260.8 11.7 %cholesky.446 = f32[128,128]{1,0:T(8,128)S(1)} custom-call(f32[128,128]{1,0:T(8,128)S(1)} %cholesky.599), custom_call_target="Cholesky" | custom-call | tf_op jit(solution)/shard_map/jit(cholesky)/cholesky | solution.py:52
  285.0 12.1 %cholesky.465 = f32[128,128]{1,0:T(8,128)S(1)} custom-call(f32[128,128]{1,0:T(8,128)S(1)} %cholesky.603), custom_call_target="Cholesky" | custom-call | tf_op jit(solution)/shard_map/jit(cholesky)/cholesky | solution.py:52
  309.8 11.7 %cholesky.486 = f32[128,128]{1,0:T(8,128)S(1)} custom-call(f32[128,128]{1,0:T(8,128)S(1)} %cholesky.608), custom_call_target="Cholesky" | custom-call | tf_op jit(solution)/shard_map/jit(cholesky)/cholesky | solution.py:52
  333.5 11.9 %cholesky.503 = f32[128,128]{1,0:T(8,128)S(1)} custom-call(f32[128,128]{1,0:T(8,128)S(1)} %convolution_subtract_fusion.14), custom_call_target="Cholesky" | custom-call | tf_op jit(solution)/shard_map/jit(cholesky)/cholesky | solution.py:52
  349.8 11.4 %while.7 = (s32[]{:T(128)}, f32[512,512]{1,0:T(8,128)}, s32[4,2]{0,1:T(2,128)S(1)}, f32[4,128,128]{2,1,0:T(8,128)S(1)}, s32[]{:T(128)}) while((s32[]{:T(128)}, f32[512,512]{1,0:T(8,128)}, s32[4,2]{0,1:T(2,128)S(1)}, f32[4,128,128]{2,1,0:T(8,128)S(1)}, s32[]{:T(128)}) %tuple.105), condition=%wide.while_cond.clone, body=%wide.while_body.clone.sunk | while | flops 2 | bytes 131181 | solution.py:53
  361.2 39.3 %custom-call.42 = f32[4,128,128]{1,2,0:T(8,128)S(1)} custom-call(f32[4,128,128]{2,1,0:T(8,128)S(1)} %get-tuple-element.27), custom_call_target="InvertDiagBlocksLowerTriangular" | custom-call | tf_op jit(solution)/shard_map/jit(_solve_triangular)/triangular_solve | solution.py:53
  422.6 94.6 %all-gather.11.cloned.1.call-done = bf16[32,128,1024]{2,1,0:T(8,128)(2,1)} async-done(((bf16[1,128,1024]{2,1,0:T(8,128)(2,1)}), bf16[32,128,1024]{2,1,0:T(8,128)(2,1)}) %all-gather.11.cloned.1.call-update) | async-done | bytes 8388624 | tf_op jit(solution)/shard_map/all_gather | solution.py:74
  535.0 10.3 %reshape.264 = f32[32,128,512]{2,1,0:T(8,128)} reshape(f32[32,1,128,4,128]{4,3,2,0,1:T(4,128)} %fusion.4) | data formatting | bytes 16777216 | tf_op jit(solution)/shard_map/reshape.65
  545.2 10.4 %fusion.2 = f32[4,128,512]{2,0,1:T(4,128)S(1)} fusion(f32[32,128,512]{2,1,0:T(8,128)} %reshape.264, s32[32]{0:T(128)S(1)} %get-tuple-element.112, pred[32]{0:T(512)(128)(4,1)S(1)} %broadcast_compare_fusion), kind=kOutput, calls=%fused_computation.8 | convolution fusion | flops 100663552 | bytes 9437344 | tf_op jit(solution)/shard_map/muvx,mut->tvx/dot_general | solution.py:34
  562.5 25.7 %all-gather.13.cloned.1.call-done = f32[1,1024,512]{1,2,0:T(8,128)} async-done(((f32[1,128,512]{1,2,0:T(8,128)}), f32[1,1024,512]{1,2,0:T(8,128)}) %all-gather.13.cloned.1.call-update) | async-done | bytes 2097168 | tf_op jit(solution)/shard_map/all_gather | solution.py:79
  591.3 11.7 %cholesky.518 = f32[128,128]{1,0:T(8,128)S(1)} custom-call(f32[128,128]{1,0:T(8,128)S(1)} %cholesky.612), custom_call_target="Cholesky" | custom-call | tf_op jit(solution)/shard_map/jit(cholesky)/cholesky | solution.py:80
  613.6 11.7 %cholesky.537 = f32[128,128]{1,0:T(8,128)S(1)} custom-call(f32[128,128]{1,0:T(8,128)S(1)} %cholesky.616), custom_call_target="Cholesky" | custom-call | tf_op jit(solution)/shard_map/jit(cholesky)/cholesky | solution.py:80
  626.7 10.0 %custom-call.44 = f32[1,128,128]{1,2,0:T(8,128)S(1)} custom-call(f32[1,128,128]{2,1,0:T(8,128)S(1)} %get-tuple-element.80), custom_call_target="InvertDiagBlocksLowerTriangular" | custom-call | tf_op jit(solution)/shard_map/jit(cholesky)/cholesky | solution.py:80
  637.3 11.7 %cholesky.558 = f32[128,128]{1,0:T(8,128)S(1)} custom-call(f32[128,128]{1,0:T(8,128)S(1)} %cholesky.621), custom_call_target="Cholesky" | custom-call | tf_op jit(solution)/shard_map/jit(cholesky)/cholesky | solution.py:80
  660.1 11.9 %cholesky.575 = f32[128,128]{1,0:T(8,128)S(1)} custom-call(f32[128,128]{1,0:T(8,128)S(1)} %convolution_subtract_fusion.13), custom_call_target="Cholesky" | custom-call | tf_op jit(solution)/shard_map/jit(cholesky)/cholesky | solution.py:80
  684.0 39.3 %custom-call.27 = f32[4,128,128]{1,2,0:T(8,128)S(1)} custom-call(f32[4,128,128]{2,1,0:T(8,128)S(1)} %get-tuple-element.19), custom_call_target="InvertDiagBlocksLowerTriangular" | custom-call | tf_op jit(solution)/shard_map/jit(_solve_triangular)/triangular_solve | solution.py:82
  (208 shorter events, 236.9 us)
Async XLA Ops:
  7.2 39.1 %all-gather.7.cloned.1.call-start = ((), (), s32[]{:S(2)}) async-start(), calls=%async_computation | async-start | bytes 4718592 | tf_op jit(solution)/shard_map/all_gather | solution.py:48
  9.1 235.1 %all-gather.9.cloned.1.call-start = ((), (), s32[]{:S(2)}) async-start(), calls=%async_computation.1 | async-start | bytes 4718592 | tf_op jit(solution)/shard_map/all_gather | solution.py:48
  55.8 1.9 copy-start
  190.7 5.7 copy-start.1
  202.9 1.6 copy-start.8
  204.3 5.1 copy-start.4
  209.4 307.9 %all-gather.11.cloned.1.call-start = ((), (), s32[]{:S(2)}) async-start(), calls=%async_computation.2 | async-start | bytes 8650752 | tf_op jit(solution)/shard_map/all_gather | solution.py:74
  253.8 1.9 copy-start.2
  259.8 1.0 copy-start.7
  400.5 5.8 copy-start.3
  415.7 2.4 copy-start.6
  415.7 3.7 copy-start.9
  416.1 5.0 copy-start.10
  416.1 5.0 copy-start.11
  416.2 6.3 copy-start.12
  419.4 168.8 %all-gather.13.cloned.1.call-start = ((), (), s32[]{:S(2)}) async-start(), calls=%async_computation.3 | async-start | bytes 2359296 | tf_op jit(solution)/shard_map/all_gather | solution.py:79
  555.7 3.5 copy-start.5
Sparse Core Ops, SparseCore 0:
  10.4 35.7 all-gather.6
  209.5 34.6 all-gather.8
  419.5 97.7 all-gather.10
  559.3 28.7 all-gather.12
where the time goes:
time: 747 us; the launch traced here: 735 us
  other arithmetic  369 us (49%)
  waiting for transfers between devices  191 us (26%)
  local copies, waits for them, and re-layouts  90.3 us (12%)
  matrix products  61.6 us (8%)
  between operations  22.8 us (3%)
    another operation x29, other arithmetic, on_device(): pivot_block = jnp.linalg.cholesky(gathered[first_col:trailing])  159 us
    all_gather x1, waiting for transfers between devices, on_device(): lax.all_gather(contribution[None], 'leaf', axis=0, tiled=True)  94.6 us
    another operation x5, other arithmetic, on_device(): jax.scipy.linalg.solve_triangular(pivot_block, gathered.T, lower=True)  79.9 us
    another operation x15, other arithmetic, on_device(): pivot_block = jnp.linalg.cholesky(stacked[:PANEL])  79.4 us
    all_gather x2, waiting for transfers between devices, on_device(): lax.all_gather(column.reshape(row_slots, 1, BLK, PANEL), 'panel', axis=1,...  70.7 us
    another operation x2, other arithmetic, on_device(): jax.scipy.linalg.solve_triangular(pivot_block, parent_rows.T, lower=True)  39.4 us
    unnamed x34, local copies, waits for them, and re-layouts  27 us
    all_gather x1, waiting for transfers between devices, on_device(): stacked = lax.all_gather(assembled[0], 'panel', axis=0, tiled=True)  25.7 us
  transfers between devices with their start and end apart: 4, of which 4 were waited for; matrix products, arithmetic and copies ran while one was open for 1% of the time, Pallas kernels for 0%

commit v1 on v0

v1 whole, which is shorter than its diff:
```python
import jax
import jax.numpy as jnp
from jax import lax
from jax.experimental import pallas as pl
from jax.experimental.pallas import tpu as pltpu
from jax.sharding import PartitionSpec as P

BLK = 128
PANEL = 512
WC = 2048
PC = 1024
CBB = 8
NB = PANEL // BLK
SUB = 8
F32 = jnp.float32
BF16 = jnp.bfloat16


def split(a):
    hi = a.astype(BF16)
    return hi, (a - hi.astype(F32)).astype(BF16)


def dot_nn(a, b):
    return lax.dot_general(a, b, (((1,), (0,)), ((), ())), preferred_element_type=F32)


def dot_nt(a, b):
    return lax.dot_general(a, b, (((1,), (1,)), ((), ())), preferred_element_type=F32)


def mm(dot, a, b):
    (ah, al), (bh, bl) = a, b
    return dot(ah, bh) + (dot(al, bh) + dot(ah, bl))


def lanes(v, j):
    return jnp.broadcast_to(v[:, j : j + 1], (SUB, BLK))


def sublanes(v, k):
    return jnp.broadcast_to(v[k : k + 1, :], (SUB, BLK))


def factor_block(block):
    groups = BLK // SUB
    rows = [block[SUB * i : SUB * (i + 1), :] for i in range(groups)]
    sub = lax.broadcasted_iota(jnp.int32, (SUB, BLK), 0)
    lane = lax.broadcasted_iota(jnp.int32, (SUB, BLK), 1)
    for g in range(groups):
        first = SUB * g
        rest = range(1, groups - g)
        inside = (lane >= first) & (lane < first + SUB)
        cols = [[lanes(rows[i], first + k) for i in range(g, groups)] for k in range(SUB)]
        head = rows[g]
        below = [jnp.where(inside, 0.0, rows[g + i]) for i in rest]
        scale = jnp.zeros((SUB, BLK), F32)
        weights = []
        pivots = []
        for k in range(SUB):
            pivot = sublanes(cols[k][0], k)
            inv_sqrt = lax.rsqrt(pivot)
            inv = 1.0 / pivot
            scale = jnp.where(sub == k, inv_sqrt, scale)
            weights.append([cols[k][i] * inv for i in rest])
            for l in range(k + 1, SUB):
                ratio = sublanes(cols[l][0], k) * inv
                for i in range(groups - g):
                    cols[l][i] = cols[l][i] - cols[k][i] * ratio
            row = jnp.where(lane == first + k, 1.0, sublanes(head, k))
            weight = jnp.where(sub > k, cols[k][0] * inv, 0.0)
            head = jnp.where((lane == first + k) & (sub > k), 0.0, head) - weight * row
            pivots.append(jnp.where((lane > first + k) & (lane < first + SUB), 0.0, row))
        for i in rest:
            acc = below[i - 1]
            for k in range(SUB):
                acc = acc - weights[k][i - 1] * pivots[k]
            rows[g + i] = acc
        rows[g] = jnp.where(lane == first + sub, 1.0, head) * scale
    return jnp.concatenate(rows, axis=0)


def invert_panel(work, inv_hi, inv_lo):
    row = lax.broadcasted_iota(jnp.int32, (BLK, BLK), 0)
    col = lax.broadcasted_iota(jnp.int32, (BLK, BLK), 1)
    lane_block = lax.broadcasted_iota(jnp.int32, (BLK, PANEL), 1) // BLK

    def step(b, carry):
        here = pl.ds(pl.multiple_of(b * BLK, BLK), BLK)
        inv = jnp.where(row >= col, factor_block(work[b, :, here]), 0.0)
        inv_parts = split(inv)
        across = mm(dot_nn, inv_parts, split(work[b]))
        across = jnp.where(lane_block == b, jnp.concatenate([inv] * NB, axis=1), across)
        across_parts = split(across)
        work[b] = across
        for i in range(1, NB):

            @pl.when(i > b)
            def _():
                below = split(mm(dot_nt, split(work[i, :, here]), inv_parts))
                kept = jnp.where(lane_block == b, 0.0, work[i])
                work[i] = kept - mm(dot_nn, below, across_parts)

        return carry

    lax.fori_loop(0, NB, step, 0)
    for i in range(NB):
        hi, lo = split(jnp.where(lane_block <= i, work[i], 0.0))
        inv_hi[i * BLK : (i + 1) * BLK, :] = hi
        inv_lo[i * BLK : (i + 1) * BLK, :] = lo


def first_kernel(pivot, inv_hi, inv_lo, work):
    for i in range(NB):
        work[i] = pivot[i]
    invert_panel(work, inv_hi, inv_lo)


def child_kernel(mid, own, inv0_hi, inv0_lo, low, factor, contribution, work, inv1_hi, inv1_lo, mid_hi, mid_lo, low_hi, low_lo):
    inv0 = (inv0_hi[...], inv0_lo[...])

    def mid_rows(i):
        return (mid_hi[i * PANEL : (i + 1) * PANEL, :], mid_lo[i * PANEL : (i + 1) * PANEL, :])

    for half in (1, 0):
        for i in range(NB // 2):
            at = half * NB + 2 * i
            rows = mid[at : at + 2, :, :PANEL].reshape(2 * BLK, PANEL)
            hi, lo = split(mm(dot_nt, split(rows), inv0))
            mid_hi[at * BLK : (at + 2) * BLK, :] = hi
            mid_lo[at * BLK : (at + 2) * BLK, :] = lo
    for i in range(NB):
        at = PANEL + i * BLK
        part = (mid_hi[at : at + BLK, :], mid_lo[at : at + BLK, :])
        work[i] = mid[NB + i, :, PANEL:] - mm(dot_nt, part, mid_rows(1))
    invert_panel(work, inv1_hi, inv1_lo)
    inv1 = (inv1_hi[...], inv1_lo[...])
    for i in range(NB):
        part = (mid_hi[i * BLK : (i + 1) * BLK, :], mid_lo[i * BLK : (i + 1) * BLK, :])
        rows = mid[i, :, PANEL:] - mm(dot_nt, part, mid_rows(1))
        hi, lo = split(mm(dot_nt, split(rows), inv1))
        low_hi[i * BLK : (i + 1) * BLK, :] = hi
        low_lo[i * BLK : (i + 1) * BLK, :] = lo
    for s in range(2):
        first = mm(dot_nt, split(own[s, :, :PANEL]), inv0)
        first_parts = split(first)
        rows = own[s, :, PANEL:PC] - mm(dot_nt, first_parts, mid_rows(1))
        second = mm(dot_nt, split(rows), inv1)
        factor[s, :, :PANEL] = first
        if s == 0:
            factor[s, :, PANEL:] = jnp.where(low[0] == 1, 0.0, second)
        else:
            factor[s, :, PANEL:] = second
            rest = own[s, :, PC : PC + PANEL] - mm(dot_nt, first_parts, mid_rows(0))
            rest = rest - mm(dot_nt, split(second), (low_hi[...], low_lo[...]))
            contribution[...] = rest.astype(BF16)


def assemble_kernel(at, parent_of, owner_slot, front_blocks, block_lists, entries, gathered, out, buf, sem):
    leaf = at[0]
    panel = at[1]

    def find(q, live):
        return jnp.where(owner_slot[q] == leaf, front_blocks[q], live)

    live = lax.fori_loop(0, owner_slot.shape[0], find, jnp.int32(0))
    for t in range(entries.shape[0]):
        alive = t * at[2] + panel < live
        out[t] = jnp.where(alive, entries[t], 0.0)

    def add(c, carry):
        @pl.when(owner_slot[parent_of[c]] == leaf)
        def _():
            copy = pltpu.make_async_copy(gathered.at[c], buf, sem)
            copy.start()
            copy.wait()
            t = block_lists[c, panel] // at[2]
            for k in range(NB):

                @pl.when(block_lists[c, k] == k)
                def _():
                    cols = slice(k * BLK, (k + 1) * BLK)
                    out[t, :, cols] = out[t, :, cols] + buf[:, cols].astype(F32)

        return carry

    lax.fori_loop(0, parent_of.shape[0], add, 0)


def parent_kernel(pivot, rows, factor, work, inv_hi, inv_lo):
    for i in range(NB):
        work[i] = pivot[i]
    invert_panel(work, inv_hi, inv_lo)
    inv = (inv_hi[...], inv_lo[...])
    for t in range(rows.shape[0]):
        factor[t] = mm(dot_nt, split(rows[t]), inv)


VMEM = pl.BlockSpec(memory_space=pltpu.VMEM)
SMEM = pl.BlockSpec(memory_space=pltpu.SMEM)
ANY = pl.BlockSpec(memory_space=pl.ANY)
PARAMS = pltpu.CompilerParams(vmem_limit_bytes=48 * 1024 * 1024)


def shape(*dims, dtype=F32):
    return jax.ShapeDtypeStruct(dims, dtype)


def gather_pivot(block):
    return lax.all_gather(block, "panel", axis=0, tiled=True)[:NB]


def exchange(contribution):
    return lax.all_gather(contribution[None], "leaf", axis=0, tiled=True)


def on_device(child_front, parent_entries, parent_of, owner_slot, front_blocks, block_lists):
    panel_count = lax.axis_size("panel")
    panel = lax.axis_index("panel")
    leaf = lax.axis_index("leaf")
    parent_slots = parent_entries.shape[1]
    own = child_front.reshape(2, BLK, WC)
    with jax.named_scope("pivot0"):
        pivot = gather_pivot(own[:1, :, :PANEL])
    with jax.named_scope("mid"):
        one = jnp.where(panel >= NB, own[0, :, :PC], own[1, :, :PC])
        mid = lax.all_gather(one[None], "panel", axis=0, tiled=True)
    inv_shapes = (shape(PANEL, PANEL, dtype=BF16), shape(PANEL, PANEL, dtype=BF16))
    work = pltpu.VMEM((NB, BLK, PANEL), F32)
    half = pltpu.VMEM((PANEL, PANEL), BF16)
    full = pltpu.VMEM((2 * PANEL, PANEL), BF16)
    inv0_hi, inv0_lo = pl.pallas_call(
        first_kernel,
        out_shape=inv_shapes,
        in_specs=[VMEM],
        out_specs=(VMEM, VMEM),
        scratch_shapes=[work],
        compiler_params=PARAMS,
        name="first_panel",
    )(pivot)
    low = (panel < NB).astype(jnp.int32).reshape(1)
    factor, contribution = pl.pallas_call(
        child_kernel,
        out_shape=(shape(2, BLK, PC), shape(BLK, PANEL, dtype=BF16)),
        in_specs=[VMEM, VMEM, VMEM, VMEM, SMEM],
        out_specs=(VMEM, VMEM),
        scratch_shapes=[work, half, half, full, full, half, half],
        compiler_params=PARAMS,
        name="child",
    )(mid, own, inv0_hi, inv0_lo, low)
    with jax.named_scope("leaf_exchange"):
        gathered = exchange(contribution)
    at = jnp.stack([leaf, panel, panel_count]).astype(jnp.int32)
    assembled = pl.pallas_call(
        assemble_kernel,
        out_shape=shape(parent_slots, BLK, PANEL),
        in_specs=[SMEM, SMEM, SMEM, SMEM, SMEM, VMEM, ANY],
        out_specs=VMEM,
        scratch_shapes=[pltpu.VMEM((BLK, PANEL), BF16), pltpu.SemaphoreType.DMA],
        compiler_params=PARAMS,
        name="assemble",
    )(at, parent_of, owner_slot, front_blocks, block_lists, parent_entries.reshape(parent_slots, BLK, PANEL), gathered)
    with jax.named_scope("pivot2"):
        stacked = gather_pivot(assembled[:1])
    parent_factor = pl.pallas_call(
        parent_kernel,
        out_shape=shape(parent_slots, BLK, PANEL),
        in_specs=[VMEM, VMEM],
        out_specs=VMEM,
        scratch_shapes=[work, half, half],
        compiler_params=PARAMS,
        name="parent",
    )(stacked, assembled)
    return (factor.reshape(child_front.shape[:-1] + (PC,)), parent_factor.reshape(parent_entries.shape))


def solution(mesh):
    front = P("leaf", None, "panel", None, None)
    return jax.shard_map(
        on_device,
        mesh=mesh,
        in_specs=(front, front, P(), P(), P(), P()),
        out_specs=(front, front),
        check_vma=False,
    )
```

time: 747 us -> 263 us (0.35); the launches traced: 735 us -> 260 us
  other arithmetic: 369 us -> 2.14 us
  Pallas kernels: 0 us -> 82.2 us
  local copies, waits for them, and re-layouts: 90.3 us -> 8.75 us
  matrix products: 61.6 us -> 0 us
  waiting for transfers between devices: 191 us -> 153 us
  between operations: 22.8 us -> 13.8 us
    another operation x51 -> x1, other arithmetic: 357 us -> 0.08 us  [on_device(): at = jnp.stack([leaf, panel, panel_count]).astype(jnp.int32)]
    pallas_call x0 -> x4, Pallas kernels: none -> 82.2 us  [the longest x1 36.7 us: on_device(): pl.pallas_call(child_kernel, out_shape=(shape(2, BLK, PC), shape(BLK, PAN...]
    another operation x53 -> x0, local copies, waits for them, and re-layouts: 38.3 us -> none  [the longest x28 19.2 us: on_device(): jax.scipy.linalg.solve_triangular(pivot_block, gathered.T, lower=True)]
    all_gather x4, waiting for transfers between devices: 191 us -> 153 us  [the longest x1 79.6 us: exchange(): return lax.all_gather(contribution[None], 'leaf', axis=0, tiled=True)]
    another operation x39 -> x0, matrix products: 36.3 us -> none  [the longest x14 24 us: on_device(): jax.scipy.linalg.solve_triangular(pivot_block, gathered.T, lower=True)]
    dot_general x4 -> x0, matrix products: 25.3 us -> none  [the longest x1 10.4 us: place_rows(): jnp.einsum('muvx,mut->tvx', placed, target, precision=lax.Precision.HIGHEST)]
    unnamed x34 -> x21, local copies, waits for them, and re-layouts: 27 us -> 3.77 us
    all_gather x2 -> x0, local copies, waits for them, and re-layouts: 10.9 us -> none  [on_device(): lax.all_gather(column.reshape(row_slots, 1, BLK, PANEL), 'panel', axis=1,...]
  transfers between devices with their start and end apart: 4 -> 4, of which waited for: 4 -> 4; matrix products, arithmetic and copies ran while one was open for 1% -> 1% of each run, Pallas kernels for 0% -> 8%
where the time goes in v1:
time: 263 us; the launch traced here: 260 us
  waiting for transfers between devices  153 us (58%)
  Pallas kernels  82.2 us (31%)
  between operations  13.8 us (5%)
  local copies, waits for them, and re-layouts  8.75 us (3%)
    all_gather x1, waiting for transfers between devices, exchange(): return lax.all_gather(contribution[None], 'leaf', axis=0, tiled=True)  79.6 us
    all_gather x2, waiting for transfers between devices, gather_pivot(): return lax.all_gather(block, 'panel', axis=0, tiled=True)[:NB]  60.5 us
    pallas_call x1, Pallas kernels, on_device(): pl.pallas_call(child_kernel, out_shape=(shape(2, BLK, PC), shape(BLK, PAN...  36.7 us
    pallas_call x1, Pallas kernels, on_device(): pl.pallas_call(parent_kernel, out_shape=shape(parent_slots, BLK, PANEL),...  23.3 us
    pallas_call x1, Pallas kernels, on_device(): pl.pallas_call(first_kernel, out_shape=inv_shapes, in_specs=[VMEM], out_s...  20.5 us
    all_gather x1, waiting for transfers between devices, on_device(): mid = lax.all_gather(one[None], 'panel', axis=0, tiled=True)  13.1 us
  transfers between devices with their start and end apart: 4, of which 4 were waited for; matrix products, arithmetic and copies ran while one was open for 1% of the time, Pallas kernels for 8%

profile of v1, /device:TPU:39, one launch (start us, length us, event | category | flops | bytes accessed | tf_op | source)
XLA Modules:
  0.0 260.4 jit_solution(10346773776766522123)
XLA Ops:
  7.2 0.0 all-gather.8.cloned.1.call-start
  7.2 1.7 slice.26
  8.9 0.0 all-gather.8.cloned.1.call-update
  8.9 0.0 all-gather.6.cloned.1.call-start
  9.0 2.1 slice_select_fusion
  11.1 0.0 all-gather.12.cloned.1.call-start
  11.1 29.1 %all-gather.8.cloned.1.call-done = f32[8,128,512]{2,1,0:T(8,128)} async-done(((f32[1,128,512]{2,1,0:T(8,128)}), f32[8,128,512]{2,1,0:T(8,128)}) %all-gather.8.cloned.1.call-update) | async-done | bytes 2097168 | tf_op jit(solution)/shard_map/pivot0/all_gather | solution.py:210
  40.2 1.3 slice.27.pivot
  41.5 20.5 %first_panel.1 = (bf16[512,512]{1,0:T(8,128)(2,1)S(1)}, bf16[512,512]{1,0:T(8,128)(2,1)S(1)}) custom-call(f32[4,128,512]{2,1,0:T(8,128)S(1)} %slice.27.pivot), custom_call_target="tpu_custom_call" | custom-call | tf_op jit(solution)/shard_map/first_panel/pallas_call | solution.py:232
  62.0 0.8 copy-done.2
  62.8 0.8 copy-done.4
  63.6 13.1 %all-gather.6.cloned.1.call-done.mid = f32[8,128,1024]{2,1,0:T(8,128)} async-done(((f32[1,128,1024]{2,1,0:T(8,128)}), f32[8,128,1024]{2,1,0:T(8,128)}) %all-gather.6.cloned.1.call-update) | async-done | bytes 4194320 | tf_op jit(solution)/shard_map/mid/all_gather | solution.py:227
  76.7 1.0 copy-done.3
  77.8 1.0 copy-done.5
  78.8 36.7 %child.1 = (f32[2,128,1024]{2,1,0:T(8,128)}, bf16[128,512]{1,0:T(8,128)(2,1)}) custom-call(f32[8,128,1024]{2,1,0:T(8,128)} %all-gather.6.cloned.1.call-done.mid, f32[2,128,2048]{2,1,0:T(8,128)S(1)} %bitcast.14, bf16[512,512]{1,0:T(8,128)(2,1)S(1)} %copy-done.3, bf16[512,512]{1,0:T(8,128)(2,1)S(1)} %copy-done.5, s32[1]{0:T(128)} %bitcast.1.low), custom_call_target="tpu_custom_call" | custom-call | tf_op jit(solution)/shard_map/child/pallas_call | solution.py:242
  115.5 0.0 all-gather.10.cloned.1.call-start
  115.6 0.1 copy.11.block_lists
  115.6 0.1 pad_add_fusion.at
  115.7 79.6 %all-gather.12.cloned.1.call-done = bf16[4096,512]{1,0:T(8,128)(2,1)} async-done(((bf16[128,512]{1,0:T(8,128)(2,1)}), bf16[4096,512]{1,0:T(8,128)(2,1)}) %all-gather.12.cloned.1.call-update) | async-done | bytes 4194320 | tf_op jit(solution)/shard_map/leaf_exchange/all_gather | solution.py:214
  195.3 1.7 assemble.1.rows
  197.1 0.7 slice.28
  197.8 31.5 %all-gather.10.cloned.1.call-done = f32[8,128,512]{2,1,0:T(8,128)} async-done(((f32[1,128,512]{2,1,0:T(8,128)}), f32[8,128,512]{2,1,0:T(8,128)}) %all-gather.10.cloned.1.call-update) | async-done | bytes 2097168 | tf_op jit(solution)/shard_map/pivot2/all_gather | solution.py:210
  229.3 1.3 slice.29.pivot
  230.6 23.3 %parent.1 = f32[4,128,512]{2,1,0:T(8,128)} custom-call(f32[4,128,512]{2,1,0:T(8,128)S(1)} %slice.29.pivot, f32[4,128,512]{2,1,0:T(8,128)S(1)} %assemble.1.rows), custom_call_target="tpu_custom_call" | custom-call | tf_op jit(solution)/shard_map/parent/pallas_call | solution.py:265
  (19 shorter events, 0.1 us)
Async XLA Ops:
  7.2 33.0 %all-gather.8.cloned.1.call-start = ((), (), s32[]{:S(2)}) async-start(), calls=%async_computation.1 | async-start | bytes 2359296 | tf_op jit(solution)/shard_map/pivot0/all_gather | solution.py:210
  8.9 67.8 %all-gather.6.cloned.1.call-start = ((), (), s32[]{:S(2)}) async-start(), calls=%async_computation | async-start | bytes 4718592 | tf_op jit(solution)/shard_map/mid/all_gather | solution.py:227
  11.0 65.7 %copy-start = (f32[1,2,1,128,2048]{4,3,2,1,0:T(8,128)S(1)}, f32[1,2,1,128,2048]{4,3,2,1,0:T(8,128)}, u32[]{:S(2)}) copy-start(f32[1,2,1,128,2048]{4,3,2,1,0:T(8,128)} %param.6) | copy-start | bytes 6291460
  11.1 184.3 %all-gather.12.cloned.1.call-start = ((), (), s32[]{:S(2)}) async-start(), calls=%async_computation.3 | async-start | bytes 4325376 | tf_op jit(solution)/shard_map/leaf_exchange/all_gather | solution.py:214
  62.0 0.8 copy-start.2
  62.8 0.8 copy-start.4
  76.7 1.0 copy-start.3
  77.8 1.0 copy-start.5
  78.8 36.8 %copy-start.9 = (s32[32,8]{0,1:T(8,128)S(1)}, s32[32,8]{0,1:T(8,128)}, u32[]{:S(2)}) copy-start(s32[32,8]{0,1:T(8,128)} %param.11) | copy-start | bytes 3076
  78.8 116.5 %copy-start.1 = (f32[1,4,1,128,512]{4,3,2,1,0:T(8,128)S(1)}, f32[1,4,1,128,512]{4,3,2,1,0:T(8,128)}, u32[]{:S(2)}) copy-start(f32[1,4,1,128,512]{4,3,2,1,0:T(8,128)} %param.7) | copy-start | bytes 3145732
  78.8 116.5 %copy-start.6 = (s32[32]{0:T(128)S(1)}, s32[32]{0:T(128)}, u32[]{:S(2)}) copy-start(s32[32]{0:T(128)} %parent_of.1) | copy-start | bytes 388
  78.8 116.5 %copy-start.7 = (s32[32]{0:T(128)S(1)}, s32[32]{0:T(128)}, u32[]{:S(2)}) copy-start(s32[32]{0:T(128)} %owner_slot.1) | copy-start | bytes 388
  78.8 116.5 %copy-start.8 = (s32[32]{0:T(128)S(1)}, s32[32]{0:T(128)}, u32[]{:S(2)}) copy-start(s32[32]{0:T(128)} %front_blocks.1) | copy-start | bytes 388
  115.5 113.8 %all-gather.10.cloned.1.call-start = ((), (), s32[]{:S(2)}) async-start(), calls=%async_computation.2 | async-start | bytes 2359296 | tf_op jit(solution)/shard_map/pivot2/all_gather | solution.py:210
Sparse Core Ops, SparseCore 0:
  10.4 29.6 all-gather.7
  42.6 34.0 all-gather.5
  115.6 79.6 all-gather.11
  197.9 31.3 all-gather.9
